TPU v7x, 32 devices: a whole 2x2x4 slice. The times are simulated.
32 devices in a mesh: ctx: 8 (over z, x), tp: 4 (over y, core).
Axes of the slice: x: 2, y: 2, z: 4, core: 2. Of those that a mesh axis runs over, the one named last changes fastest.
Arguments:
- inputs: bfloat16 [2048, 3, 4096], P('ctx', None, 'tp'), may hold values from -6 to 6
- short_filter: float32 [3, 3, 4096], P(None, None, 'tp'), may hold values from -2.5 to 2.5
- long_filter: bfloat16 [256, 128], P('tp'), may hold values from -0.5 to 0.5
- out_weight: bfloat16 [4096, 4096], P('tp'), may hold values from -0.09375 to 0.09375
- out_cotangent: bfloat16 [2048, 4096], P('ctx'), may hold values from -6 to 6
Outputs:
- result: bfloat16 [2048, 4096], P('ctx')
- grad_inputs: bfloat16 [2048, 3, 4096], P('ctx', None, 'tp')
- grad_short: float32 [3, 3, 4096], P(None, None, 'tp')
- grad_long: float32 [256, 128], P('tp')
All inputs are finite; a program needn't handle non-finite values.
Results may differ from a plain program's by a relative error of at most 0.009.
Values may be sent and summed in bfloat16 or wider, within the bound.
No kernel may reach another device: no remote copies, remote signals or barrier semaphores. Data moves between devices by JAX's collectives and lax.ppermute only.
A program may use at most 128 MiB of HBM per device.

v0:
```python
import jax
import jax.numpy as jnp
from jax import lax
from jax.sharding import PartitionSpec as P


def shifted(value, axis, steps):
    count = lax.axis_size(axis)
    initial, last = (max(0, -steps), min(count, count - steps))
    return lax.ppermute(value, axis, [(source, source + steps) for source in range(initial, last)])


def short_conv(extended, taps, count):
    span = taps.shape[0]
    total = taps[0] * extended[span - 1 : span - 1 + count]
    for lag in range(1, span):
        total = total + taps[lag] * extended[span - 1 - lag : span - 1 - lag + count]
    return total


def tap_table(filt, forward):
    span = filt.shape[1]
    row_pos = jnp.arange(span)[:, None]
    col_pos = jnp.arange(2 * span)[None, :]
    offset = row_pos - col_pos + span if forward else col_pos - row_pos
    valid = (offset >= 0) & (offset < span)
    picked = filt[:, jnp.clip(offset, 0, span - 1)]
    return jnp.where(valid[None], picked, jnp.zeros((), filt.dtype))


def block_conv(table, extended, blocks, group):
    span = table.shape[1]
    chans = extended.shape[1]
    first = extended[: blocks * span].reshape(blocks, span, chans // group, group)
    second = extended[span : (blocks + 1) * span].reshape(blocks, span, chans // group, group)
    total = jnp.einsum(
        "gij,bjgc->bigc", table[:, :, :span], first, preferred_element_type=jnp.float32
    )
    total = total + jnp.einsum(
        "gij,bjgc->bigc", table[:, :, span:], second, preferred_element_type=jnp.float32
    )
    return total.reshape(blocks * span, chans)


def rounded_term(values):
    return lax.optimization_barrier(values.astype(jnp.bfloat16)).astype(jnp.float32)


def local(inputs, short_filter, long_filter, out_weight, out_cotangent):
    count = inputs.shape[0]
    chans = inputs.shape[2]
    groups = long_filter.shape[0]
    span = long_filter.shape[1]
    lags = short_filter.shape[0]
    group = chans // groups
    blocks = count // span
    tokens_all = count * lax.axis_size("ctx")
    signal = inputs.astype(jnp.float32)
    zero_rows = jnp.zeros((lags - 1, 3, chans), jnp.float32)
    local_feat = short_conv(jnp.concatenate([zero_rows, signal], axis=0), short_filter, count)
    tail_gated = (local_feat[count - (span - 1) :, 1] * local_feat[count - (span - 1) :, 2]).astype(
        jnp.bfloat16
    )
    tail_inputs = inputs[count - (lags - 1) :].reshape(3 * (lags - 1), chans)
    sent = jnp.concatenate([tail_gated, tail_inputs], axis=0)
    taken = shifted(sent, "ctx", 1)
    gated_rim = taken[: span - 1]
    input_rim = taken[span - 1 :].reshape(lags - 1, 3, chans).astype(jnp.float32)
    signal_ext = jnp.concatenate([input_rim, signal], axis=0)
    feat = short_conv(signal_ext, short_filter, count)
    query, keyed, valued = (feat[:, 0], feat[:, 1], feat[:, 2])
    gated = (keyed * valued).astype(jnp.bfloat16)
    gated_ext = jnp.concatenate([jnp.zeros((1, chans), jnp.bfloat16), gated_rim, gated], axis=0)
    forward_table = tap_table(long_filter, True)
    mixed = block_conv(forward_table, gated_ext, blocks, group)
    gate_out = (query * mixed).astype(jnp.bfloat16)
    partial_value = rounded_term(jnp.dot(gate_out, out_weight, preferred_element_type=jnp.float32))
    result = lax.psum(partial_value.astype(jnp.bfloat16), "tp")
    grad_gate = lax.dot_general(
        out_cotangent, out_weight, (((1,), (1,)), ((), ())), preferred_element_type=jnp.float32
    )
    grad_mixed = (grad_gate * query).astype(jnp.bfloat16)
    grad_query = grad_gate * mixed
    backward_table = tap_table(long_filter, False)
    head_gated = block_conv(backward_table, grad_mixed, 1, group)[: lags - 1]
    head_feat = jnp.stack(
        [grad_query[: lags - 1], head_gated * valued[: lags - 1], head_gated * keyed[: lags - 1]],
        axis=1,
    ).astype(jnp.bfloat16)
    sent_back = jnp.concatenate(
        [grad_mixed[: span - 1], head_feat.reshape(3 * (lags - 1), chans)], axis=0
    )
    taken_back = shifted(sent_back, "ctx", -1)
    mixed_rim = taken_back[: span - 1]
    feat_rim = taken_back[span - 1 :].reshape(lags - 1, 3, chans)
    mixed_ext = jnp.concatenate(
        [grad_mixed, mixed_rim, jnp.zeros((1, chans), jnp.bfloat16)], axis=0
    )
    grad_gated = block_conv(backward_table, mixed_ext, blocks, group)
    grad_feat = jnp.stack([grad_query, grad_gated * valued, grad_gated * keyed], axis=1).astype(
        jnp.bfloat16
    )
    grad_feat_ext = lax.optimization_barrier(jnp.concatenate([grad_feat, feat_rim], axis=0)).astype(
        jnp.float32
    )
    grad_in = short_filter[0] * grad_feat_ext[:count]
    for lag in range(1, lags):
        grad_in = grad_in + short_filter[lag] * grad_feat_ext[lag : lag + count]
    grad_feat32 = grad_feat_ext[:count]
    short_rows = [
        jnp.sum(grad_feat32 * signal_ext[lags - 1 - lag : lags - 1 - lag + count], axis=0)
        for lag in range(lags)
    ]
    short_local = jnp.stack(short_rows, axis=0)
    mixed_blocks = grad_mixed.reshape(blocks, span, groups, group)
    earlier = gated_ext[:count].reshape(blocks, span, groups, group)
    current = gated_ext[span:].reshape(blocks, span, groups, group)
    products = jnp.concatenate(
        [
            jnp.einsum("bigc,bjgc->gij", mixed_blocks, earlier, preferred_element_type=jnp.float32),
            jnp.einsum("bigc,bjgc->gij", mixed_blocks, current, preferred_element_type=jnp.float32),
        ],
        axis=2,
    )
    flipped = products[:, :, ::-1].reshape(groups, 2 * span * span)
    skewed = flipped[:, span - 1 : span - 1 + span * (2 * span - 1)].reshape(
        groups, span, 2 * span - 1
    )[:, :, :span]
    long_local = jnp.sum(skewed, axis=1)
    long_total, short_total = lax.psum((long_local, short_local), "ctx")
    grad_short = short_total * float(tokens_all) ** (-0.5)
    grad_long = long_total * float(tokens_all * group) ** (-0.5)
    return (result, grad_in.astype(jnp.bfloat16), grad_short, grad_long)


def solution(mesh):
    in_specs = (
        P("ctx", None, "tp"),
        P(None, None, "tp"),
        P("tp", None),
        P("tp", None),
        P("ctx", None),
    )
    out_specs = (P("ctx", None), P("ctx", None, "tp"), P(None, None, "tp"), P("tp", None))
    return jax.shard_map(local, mesh=mesh, in_specs=in_specs, out_specs=out_specs, check_vma=False)
```

profile of v0, /device:TPU:0, one launch (start us, length us, event | category | flops | bytes accessed | tf_op | source)
XLA Modules:
  0.0 584.0 jit_solution(4579067291675489319)
XLA Ops:
  7.2 3.6 convert_element_type.48
  10.8 0.8 slice.132
  11.7 5.0 multiply_add_fusion.1
  16.7 0.1 fusion.39
  16.9 4.9 collective-permute-start
  21.9 0.1 copy.30
  22.1 115.0 %gather_fusion = bf16[32768,64]{1,0:T(8,128)(2,1)} fusion(bf16[64,128]{0,1:T(8,128)(2,1)S(1)} %copy.30, s32[32768]{0:T(1024)S(1)} %broadcast_clamp_fusion.1), kind=kCustom, calls=%fused_computation | custom fusion | bytes 8519680 | tf_op jit(solution)/shard_map/gather | solution.py:27
  137.1 10.1 %copy.63 = bf16[128,256,64]{1,0,2:T(8,128)(2,1)} copy(bf16[128,256,64]{2,1,0:T(8,128)(2,1)} %bitcast.111) | data formatting | bytes 8388608 | tf_op jit(solution)/shard_map/gather | solution.py:27
  147.3 115.0 %gather_fusion.1 = bf16[32768,64]{1,0:T(8,128)(2,1)} fusion(bf16[64,128]{0,1:T(8,128)(2,1)S(1)} %copy.30, s32[32768]{0:T(1024)S(1)} %broadcast_clamp_fusion), kind=kCustom, calls=%fused_computation.1 | custom fusion | bytes 8519680 | tf_op jit(solution)/shard_map/gather | solution.py:27
  262.3 10.1 %copy.64 = bf16[128,256,64]{1,0,2:T(8,128)(2,1)} copy(bf16[128,256,64]{2,1,0:T(8,128)(2,1)} %bitcast.110) | data formatting | bytes 8388608 | tf_op jit(solution)/shard_map/gather | solution.py:27
  272.4 4.6 select_bitcast_fusion.1
  276.9 2.2 select_bitcast_fusion
  279.2 5.0 multiply_add_fusion
  284.2 0.1 multiply_convert_fusion.5
  284.4 1.6 copy-done.3
  285.9 0.1 fusion.56
  286.1 1.0 copy.33
  287.1 1.2 convert_element_type.55
  288.3 0.9 pad_maximum_fusion.5
  289.2 2.0 copy.29
  291.2 1.2 reshape.165
  292.4 3.0 fusion.4
  295.4 2.8 fusion.23
  298.2 0.6 copy.35
  298.7 1.0 copy.88
  299.8 2.5 copy.36
  302.3 7.1 %multiply_convert_fusion.3 = (bf16[256,1024]{1,0:T(8,128)(2,1)}, bf16[256,1024]{1,0:T(8,128)(2,1)S(1)}) fusion(f32[256,1024]{1,0:T(8,128)} %copy.36, f32[256,3,1024]{2,0,1:T(8,128)} %copy-done.3, bf16[256,4096]{1,0:T(8,128)(2,1)S(1)} %copy-done, bf16[1024,4096]{1,0:T(8,128)(2,1)} %param.8), kind=kOutput, calls=%fused_computation.49 | convolution fusion | flops 2148532224 | bytes 13631488 | tf_op jit(solution)/shard_map/dot_general | solution.py:79
  309.4 0.2 copy.38
  309.7 0.1 reshape.167
  309.8 2.7 convolution_bitcast_fusion
  312.5 2.7 convolution_bitcast_fusion.1
  315.2 0.2 copy.43
  315.4 0.2 copy.42
  315.6 2.8 fusion.11
  318.4 2.8 fusion.27
  321.2 0.2 copy.65
  321.4 0.8 fusion.49
  322.3 1.3 collective-permute-start.1
  323.6 7.7 %pad_maximum_fusion = f32[64,128,256]{1,2,0:T(8,128)} fusion(f32[64,128,128]{1,2,0:T(8,128)} %convolution_bitcast_fusion, f32[64,128,128]{1,2,0:T(8,128)} %convolution_bitcast_fusion.1), kind=kLoop, calls=%fused_computation.2 | loop fusion | flops 2097152 | bytes 16777216 | tf_op jit(solution)/shard_map/concatenate | solution.py:118
  331.3 63.8 %rev.3 = f32[64,128,256]{1,2,0:T(8,128)} reverse(f32[64,128,256]{1,2,0:T(8,128)} %pad_maximum_fusion), dimensions={2} | reverse | bytes 16777216 | tf_op jit(solution)/shard_map/rev | solution.py:125
  395.2 9.2 %copy.69 = f32[8,8,128,256]{3,1,2,0:T(8,128)} copy(f32[8,8,128,256]{2,3,1,0:T(8,128)} %bitcast.108) | data formatting | bytes 16777216
  404.3 8.8 %slice.190 = f32[64,32640]{1,0:T(8,128)} slice(f32[64,32768]{1,0:T(8,128)} %bitcast.109), slice={[0:64], [127:32767]} | slice | bytes 16711680 | tf_op jit(solution)/shard_map/slice | solution.py:126
  413.2 15.9 %reshape.174 = f32[64,128,255]{2,1,0:T(8,128)} reshape(f32[64,32640]{1,0:T(8,128)} %slice.190) | data formatting | bytes 16711680 | tf_op jit(solution)/shard_map/reshape | solution.py:126
  429.1 3.3 slice_reduce_fusion
  432.5 0.2 copy.46
  432.7 0.1 reshape.170
  432.9 2.8 fusion.6
  435.6 2.8 fusion.19
  438.4 0.6 copy.48
  439.0 0.8 reshape.171
  439.8 0.3 copy.49
  440.2 1.9 multiply_convert_fusion.1
  442.1 0.1 pad_maximum_fusion.2
  442.3 0.4 convert_element_type.60
  442.7 1.5 copy-done.2
  444.1 0.5 copy-done.5
  444.6 3.1 multiply_reduce_fusion.1
  447.7 0.6 pad_maximum_fusion.9
  448.4 7.4 %convolution_convert_fusion = bf16[256,4096]{1,0:T(8,128)(2,1)} fusion(bf16[1024,4096]{1,0:T(8,128)(2,1)} %param.8, f32[256,1024]{1,0:T(8,128)S(1)} %copy-done.8, f32[256,3,1024]{2,0,1:T(8,128)} %copy-done.3), kind=kOutput, calls=%fused_computation.3 | convolution fusion | flops 2149056512 | bytes 12582912 | tf_op jit(solution)/shard_map/dot_general | solution.py:77
  455.8 64.1 %all-reduce.7.cloned.1.call-done = (f32[3,3,1024]{2,1,0:T(4,128)}, f32[64,128]{1,0:T(8,128)}) async-done(((f32[3,3,1024]{2,1,0:T(4,128)}, f32[64,128]{1,0:T(8,128)}), (f32[3,3,1024]{2,1,0:T(4,128)}, f32[64,128]{1,0:T(8,128)})) %all-reduce.7.cloned.1.call-update) | async-done | bytes 69648 | tf_op jit(solution)/shard_map/psum | solution.py:130
  519.9 1.4 broadcast_multiply_fusion.1
  521.3 1.4 broadcast_multiply_fusion
  522.7 51.3 %all-reduce.5.cloned.1.call-done = bf16[256,4096]{1,0:T(8,128)(2,1)} async-done(((bf16[256,4096]{1,0:T(8,128)(2,1)}), bf16[256,4096]{1,0:T(8,128)(2,1)}) %all-reduce.5.cloned.1.call-update) | async-done | bytes 2097168 | tf_op jit(solution)/shard_map/psum | solution.py:78
  574.0 3.1 copy.92
  (56 shorter events, 0.9 us)
Async XLA Ops:
  7.2 295.1 %copy-start = (bf16[256,4096]{1,0:T(8,128)(2,1)S(1)}, bf16[256,4096]{1,0:T(8,128)(2,1)}, u32[]{:S(2)}) copy-start(bf16[256,4096]{1,0:T(8,128)(2,1)} %param.9) | copy-start | bytes 6291460
  7.2 4.5 copy-start.10
  7.2 512.7 %all-reduce.7.cloned.1.call-start = ((), (), s32[]{:S(2)}) async-start(), calls=%async_computation.1 | async-start | bytes 163840 | tf_op jit(solution)/shard_map/psum | solution.py:130
  11.7 10.2 %copy-start.11 = (bf16[64,128]{1,0:T(8,128)(2,1)S(1)}, bf16[64,128]{1,0:T(8,128)(2,1)}, u32[]{:S(2)}) copy-start(bf16[64,128]{1,0:T(8,128)(2,1)} %param.7) | copy-start | bytes 49156
  16.9 262.3 %collective-permute-start = (bf16[133,1024]{1,0:T(8,128)(2,1)S(1)}, bf16[133,1024]{1,0:T(8,128)(2,1)S(1)}, u32[]{:S(2)}, u32[]{:S(2)}) collective-permute-start(bf16[133,1024]{1,0:T(8,128)(2,1)S(1)} %pad_maximum_fusion.7), channel_id=1, source_target_pairs={{0,4},{4,8},{8,12},{12,16},{16,20},{20,24},{24,28},{1,5},{5,9},{9,... | collective-permute-start | bytes 817160 | tf_op jit(solution)/shard_map/ppermute | solution.py:10
  272.4 4.6 copy-start.4
  284.2 1.7 copy-start.3
  292.4 5.8 copy-start.6
  309.7 2.9 copy-start.7
  315.6 6.6 %copy-start.9 = (bf16[256,1024]{1,0:T(8,128)(2,1)S(1)}, bf16[256,1024]{1,0:T(8,128)(2,1)}, u32[]{:S(2)}) copy-start(bf16[256,1024]{1,0:T(8,128)(2,1)} %get-tuple-element.14) | copy-start | bytes 1572868
  322.3 110.0 %collective-permute-start.1 = (bf16[133,1024]{1,0:T(8,128)(2,1)S(1)}, bf16[133,1024]{1,0:T(8,128)(2,1)S(1)}, u32[]{:S(2)}, u32[]{:S(2)}) collective-permute-start(bf16[133,1024]{1,0:T(8,128)(2,1)S(1)} %pad_maximum_fusion.8), channel_id=1, source_target_pairs={{4,0},{8,4},{12,8},{16,12},{20,16},{24,20},{28,24},{5,1},{9,5},{13... | collective-permute-start | bytes 817160 | tf_op jit(solution)/shard_map/ppermute | solution.py:10
  442.2 1.9 copy-start.2
  442.3 2.3 copy-start.5
  444.6 3.8 copy-start.8
  448.4 125.7 %all-reduce.5.cloned.1.call-start = ((), (), s32[]{:S(2)}) async-start(), calls=%async_computation | async-start | bytes 4194304 | tf_op jit(solution)/shard_map/psum | solution.py:78
  455.8 121.3 %copy-start.1 = (bf16[256,4096]{1,0:T(8,128)(2,1)S(1)}, bf16[256,4096]{1,0:T(8,128)(2,1)}, u32[]{:S(2)}) copy-start(bf16[256,4096]{1,0:T(8,128)(2,1)} %param.9) | copy-start | bytes 6291460
Sparse Core Ops, SparseCore 0:
  448.5 71.3 all-reduce.6
  522.8 51.1 all-reduce.4
where the time goes:
time: 590 us; the launch traced here: 584 us
  local copies, waits for them, and re-layouts  368 us (62%)
  waiting for transfers between devices  115 us (19%)
  other arithmetic  42.7 us (7%)
  matrix products  36.9 us (6%)
  between operations  14.5 us (2%)
  starting transfers between devices  6.23 us (1%)
    gather x4, local copies, waits for them, and re-layouts, tap_table(): picked = filt[:, jnp.clip(offset, 0, span - 1)]  250 us
    psum x1, waiting for transfers between devices, local(): long_total, short_total = lax.psum((long_local, short_local), 'ctx')  64.1 us
    rev x1, local copies, waits for them, and re-layouts, local(): flipped = products[:, :, ::-1].reshape(groups, 2 * span * span)  63.8 us
    psum x1, waiting for transfers between devices, local(): result = lax.psum(partial_value.astype(jnp.bfloat16), 'tp')  51.3 us
    unnamed x30, local copies, waits for them, and re-layouts  17.1 us
    reshape x1, local copies, waits for them, and re-layouts, local(): flipped[:, span - 1:span - 1 + span * (2 * span - 1)]  15.9 us
  transfers between devices with their start and end apart: 4, of which 2 were waited for; matrix products, arithmetic and copies ran while one was open for 64% of the time, Pallas kernels for 0%

commit v1 on v0

--- a/solution.py
+++ b/solution.py
@@ -75,7 +75,7 @@
     mixed = block_conv(forward_table, gated_ext, blocks, group)
     gate_out = (query * mixed).astype(jnp.bfloat16)
     partial_value = rounded_term(jnp.dot(gate_out, out_weight, preferred_element_type=jnp.float32))
-    result = lax.psum(partial_value.astype(jnp.bfloat16), "tp")
+    result = jnp.sum(lax.all_gather(partial_value.astype(jnp.bfloat16), "tp"), axis=0)
     grad_gate = lax.dot_general(
         out_cotangent, out_weight, (((1,), (1,)), ((), ())), preferred_element_type=jnp.float32
     )

time: 590 us -> 544 us (0.922)
  waiting for transfers between devices: 115 us -> 63.8 us
  other arithmetic: 42.7 us -> 49.7 us
    psum x1 -> x0, waiting for transfers between devices: 51.3 us -> none  [local(): result = lax.psum(partial_value.astype(jnp.bfloat16), 'tp')]
    reduce_sum x0 -> x1, other arithmetic: none -> 7.03 us  [local(): jnp.sum(lax.all_gather(partial_value.astype(jnp.bfloat16), 'tp'), axis=0)]
    unnamed x30 -> x29, local copies, waits for them, and re-layouts: 17.1 us -> 14 us
  transfers between devices with their start and end apart: 4 -> 4, of which waited for: 2 -> 1; matrix products, arithmetic and copies ran while one was open for 64% -> 70% of each run, Pallas kernels for 0% -> 0%
where the time goes in v1:
time: 544 us; the launch traced here: 538 us
  local copies, waits for them, and re-layouts  365 us (67%)
  waiting for transfers between devices  63.8 us (12%)
  other arithmetic  49.7 us (9%)
  matrix products  36.9 us (7%)
  between operations  15.9 us (3%)
  starting transfers between devices  6.49 us (1%)
    gather x4, local copies, waits for them, and re-layouts, tap_table(): picked = filt[:, jnp.clip(offset, 0, span - 1)]  250 us
    rev x1, local copies, waits for them, and re-layouts, local(): flipped = products[:, :, ::-1].reshape(groups, 2 * span * span)  63.8 us
    psum x1, waiting for transfers between devices, local(): long_total, short_total = lax.psum((long_local, short_local), 'ctx')  63.8 us
    reshape x1, local copies, waits for them, and re-layouts, local(): flipped[:, span - 1:span - 1 + span * (2 * span - 1)]  15.9 us
    unnamed x29, local copies, waits for them, and re-layouts  14 us
  transfers between devices with their start and end apart: 4, of which 1 were waited for; matrix products, arithmetic and copies ran while one was open for 70% of the time, Pallas kernels for 0%

profile of v1, /device:TPU:0, one launch (start us, length us, event | category | flops | bytes accessed | tf_op | source)
XLA Modules:
  0.0 538.0 jit_solution(17421245676644211805)
XLA Ops:
  8.1 3.6 convert_element_type.50
  11.7 0.8 slice.132
  12.6 5.0 multiply_add_fusion.1
  17.6 0.1 fusion.39
  17.7 4.9 collective-permute-start
  22.8 0.1 copy.30
  23.0 115.0 %gather_fusion = bf16[32768,64]{1,0:T(8,128)(2,1)} fusion(bf16[64,128]{0,1:T(8,128)(2,1)S(1)} %copy.30, s32[32768]{0:T(1024)S(1)} %broadcast_clamp_fusion.1), kind=kCustom, calls=%fused_computation | custom fusion | bytes 8519680 | tf_op jit(solution)/shard_map/gather | solution.py:27
  138.0 10.1 %copy.63 = bf16[128,256,64]{1,0,2:T(8,128)(2,1)} copy(bf16[128,256,64]{2,1,0:T(8,128)(2,1)} %bitcast.112) | data formatting | bytes 8388608 | tf_op jit(solution)/shard_map/gather | solution.py:27
  148.1 115.0 %gather_fusion.1 = bf16[32768,64]{1,0:T(8,128)(2,1)} fusion(bf16[64,128]{0,1:T(8,128)(2,1)S(1)} %copy.30, s32[32768]{0:T(1024)S(1)} %broadcast_clamp_fusion), kind=kCustom, calls=%fused_computation.1 | custom fusion | bytes 8519680 | tf_op jit(solution)/shard_map/gather | solution.py:27
  263.1 10.1 %copy.64 = bf16[128,256,64]{1,0,2:T(8,128)(2,1)} copy(bf16[128,256,64]{2,1,0:T(8,128)(2,1)} %bitcast.111) | data formatting | bytes 8388608 | tf_op jit(solution)/shard_map/gather | solution.py:27
  273.2 4.6 select_bitcast_fusion.1
  277.8 2.2 select_bitcast_fusion
  280.1 5.0 multiply_add_fusion
  285.1 0.1 multiply_convert_fusion.5
  285.2 1.6 copy-done.3
  286.8 0.1 fusion.56
  286.9 1.0 copy.33
  287.9 1.2 convert_element_type.57
  289.1 0.9 pad_maximum_fusion.5
  290.0 2.0 copy.29
  292.0 1.2 reshape.165
  293.2 3.0 fusion.4
  296.2 2.8 fusion.23
  299.0 0.6 copy.35
  299.5 1.0 copy.88
  300.6 2.5 copy.36
  303.1 7.1 %multiply_convert_fusion.3 = (bf16[256,1024]{1,0:T(8,128)(2,1)}, bf16[256,1024]{1,0:T(8,128)(2,1)S(1)}) fusion(f32[256,1024]{1,0:T(8,128)} %copy.36, f32[256,3,1024]{2,0,1:T(8,128)} %copy-done.3, bf16[256,4096]{1,0:T(8,128)(2,1)S(1)} %copy-done, bf16[1024,4096]{1,0:T(8,128)(2,1)} %param.8), kind=kOutput, calls=%fused_computation.49 | convolution fusion | flops 2148532224 | bytes 13631488 | tf_op jit(solution)/shard_map/dot_general | solution.py:79
  310.3 0.2 copy.38
  310.5 0.1 reshape.167
  310.6 2.7 convolution_bitcast_fusion
  313.4 2.7 convolution_bitcast_fusion.1
  316.1 0.2 copy.43
  316.2 0.2 copy.42
  316.4 2.8 fusion.11
  319.2 2.8 fusion.27
  322.0 0.2 copy.65
  322.3 0.8 fusion.49
  323.2 1.3 collective-permute-start.1
  324.5 7.7 %pad_maximum_fusion = f32[64,128,256]{1,2,0:T(8,128)} fusion(f32[64,128,128]{1,2,0:T(8,128)} %convolution_bitcast_fusion, f32[64,128,128]{1,2,0:T(8,128)} %convolution_bitcast_fusion.1), kind=kLoop, calls=%fused_computation.2 | loop fusion | flops 2097152 | bytes 16777216 | tf_op jit(solution)/shard_map/concatenate | solution.py:118
  332.2 63.8 %rev.3 = f32[64,128,256]{1,2,0:T(8,128)} reverse(f32[64,128,256]{1,2,0:T(8,128)} %pad_maximum_fusion), dimensions={2} | reverse | bytes 16777216 | tf_op jit(solution)/shard_map/rev | solution.py:125
  396.0 9.2 %copy.69 = f32[8,8,128,256]{3,1,2,0:T(8,128)} copy(f32[8,8,128,256]{2,3,1,0:T(8,128)} %bitcast.109) | data formatting | bytes 16777216
  405.2 8.8 %slice.190 = f32[64,32640]{1,0:T(8,128)} slice(f32[64,32768]{1,0:T(8,128)} %bitcast.110), slice={[0:64], [127:32767]} | slice | bytes 16711680 | tf_op jit(solution)/shard_map/slice | solution.py:126
  414.0 15.9 %reshape.174 = f32[64,128,255]{2,1,0:T(8,128)} reshape(f32[64,32640]{1,0:T(8,128)} %slice.190) | data formatting | bytes 16711680 | tf_op jit(solution)/shard_map/reshape | solution.py:126
  429.9 3.3 slice_reduce_fusion
  433.3 0.2 copy.46
  433.6 0.1 reshape.170
  433.7 2.8 fusion.6
  436.5 2.8 fusion.19
  439.3 0.6 copy.48
  439.8 0.8 reshape.171
  440.7 0.3 copy.49
  441.0 1.9 multiply_convert_fusion.1
  442.9 0.1 pad_maximum_fusion.2
  443.1 0.4 convert_element_type.62
  443.5 1.5 copy-done.2
  445.0 0.5 copy-done.5
  445.4 3.1 multiply_reduce_fusion.1
  448.5 0.6 pad_maximum_fusion.9
  449.2 0.3 all-gather.3.cloned.1.call-start
  449.5 7.4 %convolution_convert_fusion = bf16[256,4096]{1,0:T(8,128)(2,1)} fusion(bf16[1024,4096]{1,0:T(8,128)(2,1)} %param.8, f32[256,1024]{1,0:T(8,128)S(1)} %copy-done.8, f32[256,3,1024]{2,0,1:T(8,128)} %copy-done.3), kind=kOutput, calls=%fused_computation.3 | convolution fusion | flops 2149056512 | bytes 12582912 | tf_op jit(solution)/shard_map/dot_general | solution.py:77
  456.9 63.8 %all-reduce.4.cloned.1.call-done = (f32[3,3,1024]{2,1,0:T(4,128)}, f32[64,128]{1,0:T(8,128)}) async-done(((f32[3,3,1024]{2,1,0:T(4,128)}, f32[64,128]{1,0:T(8,128)}), (f32[3,3,1024]{2,1,0:T(4,128)}, f32[64,128]{1,0:T(8,128)})) %all-reduce.4.cloned.1.call-update) | async-done | bytes 69648 | tf_op jit(solution)/shard_map/psum | solution.py:130
  520.7 1.4 broadcast_multiply_fusion.1
  522.1 1.4 broadcast_multiply_fusion
  523.5 7.0 %reduce_sum.48 = bf16[256,4096]{1,0:T(8,128)(2,1)} reduce(bf16[4,256,4096]{2,1,0:T(8,128)(2,1)} %bitcast.113, bf16[]{:T(256)} %constant.8.clone.1), dimensions={0}, to_apply=%region_0.1 | reduce | flops 3145728 | bytes 10485762 | tf_op jit(solution)/shard_map/reduce_sum | solution.py:78
  (56 shorter events, 0.8 us)
Async XLA Ops:
  8.0 295.1 %copy-start = (bf16[256,4096]{1,0:T(8,128)(2,1)S(1)}, bf16[256,4096]{1,0:T(8,128)(2,1)}, u32[]{:S(2)}) copy-start(bf16[256,4096]{1,0:T(8,128)(2,1)} %param.9) | copy-start | bytes 6291460
  8.0 4.5 copy-start.10
  8.0 512.7 %all-reduce.4.cloned.1.call-start = ((), (), s32[]{:S(2)}) async-start(), calls=%async_computation.1 | async-start | bytes 163840 | tf_op jit(solution)/shard_map/psum | solution.py:130
  12.6 10.2 %copy-start.11 = (bf16[64,128]{1,0:T(8,128)(2,1)S(1)}, bf16[64,128]{1,0:T(8,128)(2,1)}, u32[]{:S(2)}) copy-start(bf16[64,128]{1,0:T(8,128)(2,1)} %param.7) | copy-start | bytes 49156
  17.7 262.3 %collective-permute-start = (bf16[133,1024]{1,0:T(8,128)(2,1)S(1)}, bf16[133,1024]{1,0:T(8,128)(2,1)S(1)}, u32[]{:S(2)}, u32[]{:S(2)}) collective-permute-start(bf16[133,1024]{1,0:T(8,128)(2,1)S(1)} %pad_maximum_fusion.7), channel_id=1, source_target_pairs={{0,4},{4,8},{8,12},{12,16},{16,20},{20,24},{24,28},{1,5},{5,9},{9,... | collective-permute-start | bytes 817160 | tf_op jit(solution)/shard_map/ppermute | solution.py:10
  273.2 4.6 copy-start.4
  285.1 1.7 copy-start.3
  293.2 5.8 %copy-start.6 = (bf16[2,128,64,16]{1,0,3,2:T(2,128)(2,1)}, bf16[2,128,64,16]{1,0,3,2:T(2,128)(2,1)S(1)}, u32[]{:S(2)}) copy-start(bf16[2,128,64,16]{1,0,3,2:T(2,128)(2,1)S(1)} %reshape.165) | copy-start | bytes 1572868
  310.5 2.9 copy-start.7
  316.4 6.6 %copy-start.9 = (bf16[256,1024]{1,0:T(8,128)(2,1)S(1)}, bf16[256,1024]{1,0:T(8,128)(2,1)}, u32[]{:S(2)}) copy-start(bf16[256,1024]{1,0:T(8,128)(2,1)} %get-tuple-element.14) | copy-start | bytes 1572868
  323.2 110.0 %collective-permute-start.1 = (bf16[133,1024]{1,0:T(8,128)(2,1)S(1)}, bf16[133,1024]{1,0:T(8,128)(2,1)S(1)}, u32[]{:S(2)}, u32[]{:S(2)}) collective-permute-start(bf16[133,1024]{1,0:T(8,128)(2,1)S(1)} %pad_maximum_fusion.8), channel_id=1, source_target_pairs={{4,0},{8,4},{12,8},{16,12},{20,16},{24,20},{28,24},{5,1},{9,5},{13... | collective-permute-start | bytes 817160 | tf_op jit(solution)/shard_map/ppermute | solution.py:10
  443.1 1.9 copy-start.2
  443.1 2.3 copy-start.5
  445.4 4.1 copy-start.8
  449.2 74.3 %all-gather.3.cloned.1.call-start = ((), (), s32[]{:S(2)}) async-start(), calls=%async_computation | async-start | bytes 10485760 | tf_op jit(solution)/shard_map/all_gather | solution.py:78
  523.5 7.0 %copy-start.1 = (bf16[256,4096]{1,0:T(8,128)(2,1)S(1)}, bf16[256,4096]{1,0:T(8,128)(2,1)}, u32[]{:S(2)}) copy-start(bf16[256,4096]{1,0:T(8,128)(2,1)} %param.9) | copy-start | bytes 6291460
Sparse Core Ops, SparseCore 0:
  449.3 71.3 all-reduce.3
Sparse Core Ops, SparseCore 1:
  457.0 60.5 all-gather.2
